TPU v7x, 128 devices: a whole 4x4x4 slice. The times are simulated.
128 devices in a mesh: row: 8 (over y, core), col: 16 (over x, z).
Axes of the slice: x: 4, y: 4, z: 4, core: 2. Of those that a mesh axis runs over, the one named last changes fastest.
Arguments:
- tile_data: float32 [8, 16, 288, 128, 128], P('row', 'col'), as said below
- tile_rows: int32 [8, 16, 288], P('row', 'col'), may hold values from 0 to 2047, as said below
- tile_cols: int32 [8, 16, 288], P('row', 'col'), may hold values from 0 to 1023, as said below
- tile_counts: int32 [8, 16], P('row', 'col'), may hold values from 128 to 288, as said below
Outputs:
- row_scale: float32 [2097152], P('row')
- column_scale: float32 [2097152], P('col')
Inputs may be any that keep to these rules, and one draw needn't show every extreme that they name: `tile_rows`: within one device the blocks of the slots are all different. Slot k < 128 of device (p, q) holds row block q * 128 + k and column block p * 128 + k, so every row and column of A meets a used slot. `tile_cols`: column blocks of the slots, as above. `tile_counts`: some device uses all 288 slots in every draw. `tile_data`: entries are nonzero reals whose tiles have row and column scales of differing sizes.
All inputs are finite; a program needn't handle non-finite values.
Results may differ from a plain program's by a relative error of at most 0.0001.
Values sent between devices are 32-bit elements; how exact they have to be, the bound alone decides.
A program may use at most 64 MiB of HBM per device.

v0:
```python
import jax
import jax.numpy as jnp
from jax import lax
from jax.sharding import PartitionSpec as P

DIAG = 128
SWEEPS = 4
epsilon = 1e-06


def local_terms(magnitude, row_blocks, column_blocks, row_scale, column_scale, want_peak):
    scaled = magnitude * row_scale[row_blocks][:, :, None] * column_scale[column_blocks][:, None, :]
    if want_peak:
        return (scaled.max(axis=2), scaled.max(axis=1))
    return (scaled.sum(axis=2), scaled.sum(axis=1))


def peak_rows(terms, row_blocks, length):
    empty = jnp.zeros((length, terms.shape[1]), jnp.float32)
    return lax.pmax(empty.at[row_blocks].max(terms), "col")


def peak_columns(terms, column_blocks, length):
    empty = jnp.zeros((length, terms.shape[1]), jnp.float32)
    return lax.pmax(empty.at[column_blocks].max(terms), "row")


def total_rows(terms, row_blocks, length):
    empty = jnp.zeros((length, terms.shape[1]), jnp.float32)
    return lax.psum(empty.at[row_blocks].add(terms), "col")


def total_columns(terms, column_blocks, length):
    empty = jnp.zeros((length, terms.shape[1]), jnp.float32)
    return lax.psum(empty.at[column_blocks].add(terms), "row")


def on_device(tile_data, tile_rows, tile_cols, tile_counts):
    blocks = tile_data[0, 0]
    row_blocks = tile_rows[0, 0]
    column_blocks = tile_cols[0, 0]
    used_count = tile_counts[0, 0]
    slots = blocks.shape[0]
    side = blocks.shape[1]
    row_length = DIAG * lax.axis_size("col")
    column_length = DIAG * lax.axis_size("row")
    in_use = jnp.arange(slots, dtype=jnp.int32) < used_count
    magnitude = jnp.where(in_use[:, None, None], jnp.abs(blocks), jnp.float32(0.0))
    row_scale = jnp.ones((row_length, side), jnp.float32)
    column_scale = jnp.ones((column_length, side), jnp.float32)
    for sweep in range(SWEEPS):
        row_terms, column_terms = local_terms(
            magnitude, row_blocks, column_blocks, row_scale, column_scale, True
        )
        peak_row = peak_rows(row_terms, row_blocks, row_length)
        peak_col = peak_columns(column_terms, column_blocks, column_length)
        row_scale = row_scale * lax.rsqrt(peak_row + epsilon)
        column_scale = column_scale * lax.rsqrt(peak_col + epsilon)
    row_terms, column_terms = local_terms(
        magnitude, row_blocks, column_blocks, row_scale, column_scale, False
    )
    total_row = total_rows(row_terms, row_blocks, row_length)
    total_col = total_columns(column_terms, column_blocks, column_length)
    row_scale = row_scale * lax.rsqrt(total_row + epsilon)
    column_scale = column_scale * lax.rsqrt(total_col + epsilon)
    return (row_scale.reshape(-1), column_scale.reshape(-1))


def solution(mesh):
    placed = (
        P("row", "col", None, None, None),
        P("row", "col", None),
        P("row", "col", None),
        P("row", "col"),
    )
    return jax.shard_map(
        on_device, mesh=mesh, in_specs=placed, out_specs=(P("row"), P("col")), check_vma=False
    )
```

profile of v0, /device:TPU:0, one launch (start us, length us, event | category | flops | bytes accessed | tf_op | source)
XLA Modules:
  0.0 876.4 jit_solution(11298934996179545294)
XLA Ops:
  7.9 0.7 fusion.30
  8.6 0.7 fusion.31
  9.3 1.1 gather_fusion.1
  10.5 1.1 gather_fusion
  11.6 15.0 %fusion.1 = (f32[288,128]{1,0:T(8,128)S(1)}, f32[288,128]{1,0:T(8,128)S(1)}) fusion(f32[288,128]{1,0:T(8,128)S(1)} %gather_fusion.1, f32[288,128]{1,0:T(8,128)S(1)} %gather_fusion, f32[1,1,288,128,128]{4,3,2,1,0:T(8,128)} %param.4, pred[288]{0:T(512)(128)(4,1)S(1)} %iota_compare_fusion), kind=kLoop, calls=%fused_computation.27 | loop fusion | flops 28237824 | bytes 19464480 | tf_op jit(solution)/shard_map/reduce_max | solution.py:14
  26.6 2.3 scatter_custom_fusion.1
  29.0 2.5 scatter_custom_fusion
  31.6 61.3 %all-reduce.13.cloned.1.call-done = f32[1024,128]{1,0:T(8,128)} async-done(((f32[1024,128]{1,0:T(8,128)}), f32[1024,128]{1,0:T(8,128)}) %all-reduce.13.cloned.1.call-update) | async-done | bytes 524304 | tf_op jit(solution)/shard_map/pmax | solution.py:25
  92.9 1.2 add_rsqrt_fusion.1
  94.1 1.1 gather_fusion.3
  95.2 88.2 %all-reduce.11.cloned.1.call-done = f32[2048,128]{1,0:T(8,128)} async-done(((f32[2048,128]{1,0:T(8,128)}), f32[2048,128]{1,0:T(8,128)}) %all-reduce.11.cloned.1.call-update) | async-done | bytes 1048592 | tf_op jit(solution)/shard_map/pmax | solution.py:20
  183.4 1.5 add_rsqrt_fusion
  184.9 1.1 gather_fusion.2
  185.9 15.0 %fusion.2 = (f32[288,128]{1,0:T(8,128)S(1)}, f32[288,128]{1,0:T(8,128)S(1)}) fusion(f32[288,128]{1,0:T(8,128)S(1)} %gather_fusion.3, f32[288,128]{1,0:T(8,128)S(1)} %gather_fusion.2, f32[1,1,288,128,128]{4,3,2,1,0:T(8,128)} %param.4, pred[288]{0:T(512)(128)(4,1)S(1)} %iota_compare_fusion), kind=kLoop, calls=%fused_computation.28 | loop fusion | flops 28237824 | bytes 19464480 | tf_op jit(solution)/shard_map/reduce_max | solution.py:14
  201.0 2.3 scatter_custom_fusion.3
  203.4 2.5 scatter_custom_fusion.2
  205.9 58.1 %all-reduce.17.cloned.1.call-done = f32[1024,128]{1,0:T(8,128)} async-done(((f32[1024,128]{1,0:T(8,128)}), f32[1024,128]{1,0:T(8,128)}) %all-reduce.17.cloned.1.call-update) | async-done | bytes 524304 | tf_op jit(solution)/shard_map/pmax | solution.py:25
  264.0 1.2 rsqrt_multiply_fusion.5
  265.2 1.1 gather_fusion.5
  266.3 88.1 %all-reduce.15.cloned.1.call-done = f32[2048,128]{1,0:T(8,128)} async-done(((f32[2048,128]{1,0:T(8,128)}), f32[2048,128]{1,0:T(8,128)}) %all-reduce.15.cloned.1.call-update) | async-done | bytes 1048592 | tf_op jit(solution)/shard_map/pmax | solution.py:20
  354.4 1.5 rsqrt_multiply_fusion.2
  355.9 1.1 gather_fusion.4
  357.0 15.0 %fusion.4 = (f32[288,128]{1,0:T(8,128)S(1)}, f32[288,128]{1,0:T(8,128)S(1)}) fusion(f32[288,128]{1,0:T(8,128)S(1)} %gather_fusion.5, f32[288,128]{1,0:T(8,128)S(1)} %gather_fusion.4, f32[1,1,288,128,128]{4,3,2,1,0:T(8,128)} %param.4, pred[288]{0:T(512)(128)(4,1)S(1)} %iota_compare_fusion), kind=kLoop, calls=%fused_computation.30 | loop fusion | flops 28237824 | bytes 19464480 | tf_op jit(solution)/shard_map/reduce_max | solution.py:14
  372.0 2.3 scatter_custom_fusion.5
  374.3 0.2 all-reduce.19.cloned.1.call-start
  374.6 2.5 scatter_custom_fusion.4
  377.2 57.9 %all-reduce.21.cloned.1.call-done = f32[1024,128]{1,0:T(8,128)} async-done(((f32[1024,128]{1,0:T(8,128)}), f32[1024,128]{1,0:T(8,128)}) %all-reduce.21.cloned.1.call-update) | async-done | bytes 524304 | tf_op jit(solution)/shard_map/pmax | solution.py:25
  435.1 1.1 rsqrt_multiply_fusion.4
  436.2 1.1 gather_fusion.7
  437.2 88.2 %all-reduce.19.cloned.1.call-done = f32[2048,128]{1,0:T(8,128)} async-done(((f32[2048,128]{1,0:T(8,128)}), f32[2048,128]{1,0:T(8,128)}) %all-reduce.19.cloned.1.call-update) | async-done | bytes 1048592 | tf_op jit(solution)/shard_map/pmax | solution.py:20
  525.4 1.4 rsqrt_multiply_fusion.1
  526.8 1.1 gather_fusion.6
  527.8 15.0 %fusion.6 = (f32[288,128]{1,0:T(8,128)S(1)}, f32[288,128]{1,0:T(8,128)S(1)}) fusion(f32[288,128]{1,0:T(8,128)S(1)} %gather_fusion.7, f32[288,128]{1,0:T(8,128)S(1)} %gather_fusion.6, f32[1,1,288,128,128]{4,3,2,1,0:T(8,128)} %param.4, pred[288]{0:T(512)(128)(4,1)S(1)} %iota_compare_fusion), kind=kLoop, calls=%fused_computation.32 | loop fusion | flops 28237824 | bytes 19464480 | tf_op jit(solution)/shard_map/reduce_max | solution.py:14
  542.9 2.3 scatter_custom_fusion.7
  545.3 2.5 scatter_custom_fusion.6
  547.9 58.1 %all-reduce.25.cloned.1.call-done = f32[1024,128]{1,0:T(8,128)} async-done(((f32[1024,128]{1,0:T(8,128)}), f32[1024,128]{1,0:T(8,128)}) %all-reduce.25.cloned.1.call-update) | async-done | bytes 524304 | tf_op jit(solution)/shard_map/pmax | solution.py:25
  605.9 1.1 rsqrt_multiply_fusion.3
  607.1 1.1 gather_fusion.9
  608.1 88.3 %all-reduce.23.cloned.1.call-done = f32[2048,128]{1,0:T(8,128)} async-done(((f32[2048,128]{1,0:T(8,128)}), f32[2048,128]{1,0:T(8,128)}) %all-reduce.23.cloned.1.call-update) | async-done | bytes 1048592 | tf_op jit(solution)/shard_map/pmax | solution.py:20
  696.4 1.4 rsqrt_multiply_fusion
  697.8 1.1 gather_fusion.8
  698.9 15.1 %fusion.8 = (f32[288,128]{1,0:T(8,128)S(1)}, f32[288,128]{1,0:T(8,128)S(1)}) fusion(f32[288,128]{1,0:T(8,128)S(1)} %gather_fusion.9, f32[288,128]{1,0:T(8,128)S(1)} %gather_fusion.8, f32[1,1,288,128,128]{4,3,2,1,0:T(8,128)} %param.4, pred[288]{0:T(512)(128)(4,1)S(1)} %iota_compare_fusion), kind=kLoop, calls=%fused_computation.34 | loop fusion | flops 28237824 | bytes 19464480 | tf_op jit(solution)/shard_map/reduce_sum | solution.py:15
  714.0 2.3 scatter_custom_fusion.9
  716.4 2.5 scatter_custom_fusion.8
  718.9 58.0 %all-reduce.29.cloned.1.call-done = f32[1024,128]{1,0:T(8,128)} async-done(((f32[1024,128]{1,0:T(8,128)}), f32[1024,128]{1,0:T(8,128)}) %all-reduce.29.cloned.1.call-update) | async-done | bytes 524304 | tf_op jit(solution)/shard_map/psum | solution.py:35
  776.9 1.9 multiply_bitcast_fusion.1
  778.8 88.4 %all-reduce.27.cloned.1.call-done = f32[2048,128]{1,0:T(8,128)} async-done(((f32[2048,128]{1,0:T(8,128)}), f32[2048,128]{1,0:T(8,128)}) %all-reduce.27.cloned.1.call-update) | async-done | bytes 1048592 | tf_op jit(solution)/shard_map/psum | solution.py:30
  867.2 2.3 multiply_bitcast_fusion
  (28 shorter events, 0.7 us)
Async XLA Ops:
  7.2 85.7 %all-reduce.13.cloned.1.call-start = ((), (), s32[]{:S(2)}) async-start(), calls=%async_computation.1 | async-start | bytes 1048576 | tf_op jit(solution)/shard_map/pmax | solution.py:25
  28.9 154.5 %all-reduce.11.cloned.1.call-start = ((), (), s32[]{:S(2)}) async-start(), calls=%async_computation | async-start | bytes 2097152 | tf_op jit(solution)/shard_map/pmax | solution.py:20
  31.5 232.5 %all-reduce.17.cloned.1.call-start = ((), (), s32[]{:S(2)}) async-start(), calls=%async_computation.3 | async-start | bytes 1048576 | tf_op jit(solution)/shard_map/pmax | solution.py:25
  92.9 171.1 %copy-start.1 = (f32[1024,128]{1,0:T(8,128)S(1)}, f32[1024,128]{1,0:T(8,128)}, u32[]{:S(2)}) copy-start(f32[1024,128]{1,0:T(8,128)} %all-reduce.13.cloned.1.call-done) | copy-start | bytes 1572868
  183.4 171.0 %copy-start = (f32[2048,128]{1,0:T(8,128)S(1)}, f32[2048,128]{1,0:T(8,128)}, u32[]{:S(2)}) copy-start(f32[2048,128]{1,0:T(8,128)} %all-reduce.11.cloned.1.call-done) | copy-start | bytes 3145732
  203.3 151.1 %all-reduce.15.cloned.1.call-start = ((), (), s32[]{:S(2)}) async-start(), calls=%async_computation.2 | async-start | bytes 2097152 | tf_op jit(solution)/shard_map/pmax | solution.py:20
  205.9 229.2 %all-reduce.21.cloned.1.call-start = ((), (), s32[]{:S(2)}) async-start(), calls=%async_computation.5 | async-start | bytes 1048576 | tf_op jit(solution)/shard_map/pmax | solution.py:25
  374.3 151.1 %all-reduce.19.cloned.1.call-start = ((), (), s32[]{:S(2)}) async-start(), calls=%async_computation.4 | async-start | bytes 2097152 | tf_op jit(solution)/shard_map/pmax | solution.py:20
  377.1 228.8 %all-reduce.25.cloned.1.call-start = ((), (), s32[]{:S(2)}) async-start(), calls=%async_computation.7 | async-start | bytes 1048576 | tf_op jit(solution)/shard_map/pmax | solution.py:25
  545.2 151.2 %all-reduce.23.cloned.1.call-start = ((), (), s32[]{:S(2)}) async-start(), calls=%async_computation.6 | async-start | bytes 2097152 | tf_op jit(solution)/shard_map/pmax | solution.py:20
  547.8 229.1 %all-reduce.29.cloned.1.call-start = ((), (), s32[]{:S(2)}) async-start(), calls=%async_computation.9 | async-start | bytes 1048576 | tf_op jit(solution)/shard_map/psum | solution.py:35
  716.3 150.9 %all-reduce.27.cloned.1.call-start = ((), (), s32[]{:S(2)}) async-start(), calls=%async_computation.8 | async-start | bytes 2097152 | tf_op jit(solution)/shard_map/psum | solution.py:30
Sparse Core Ops, SparseCore 0:
  29.1 63.8 all-reduce.12
  96.7 86.6 all-reduce.10
  203.4 60.5 all-reduce.16
  267.7 86.6 all-reduce.14
  374.5 60.5 all-reduce.20
  438.7 86.6 all-reduce.18
  545.3 60.5 all-reduce.24
  609.8 86.6 all-reduce.22
  716.4 60.3 all-reduce.28
  780.6 86.5 all-reduce.26
where the time goes:
time: 877 us; the launch traced here: 876 us
  waiting for transfers between devices  735 us (84%)
  other arithmetic  115 us (13%)
  between operations  15 us (2%)
  local copies, waits for them, and re-layouts  10.7 us (1%)
    pmax x4, waiting for transfers between devices, peak_rows(): return lax.pmax(empty.at[row_blocks].max(terms), 'col')  353 us
    pmax x4, waiting for transfers between devices, peak_columns(): return lax.pmax(empty.at[column_blocks].max(terms), 'row')  235 us
    psum x1, waiting for transfers between devices, total_rows(): return lax.psum(empty.at[row_blocks].add(terms), 'col')  88.4 us
    reduce_max x4, other arithmetic, local_terms(): return (scaled.max(axis=2), scaled.max(axis=1))  60.2 us
    psum x1, waiting for transfers between devices, total_columns(): return lax.psum(empty.at[column_blocks].add(terms), 'row')  58 us
  transfers between devices with their start and end apart: 10, of which 10 were waited for; matrix products, arithmetic and copies ran while one was open for 3% of the time, Pallas kernels for 0%

commit v1 on v0

--- a/solution.py
+++ b/solution.py
@@ -27,7 +27,7 @@
 
 def total_rows(terms, row_blocks, length):
     empty = jnp.zeros((length, terms.shape[1]), jnp.float32)
-    return lax.psum(empty.at[row_blocks].add(terms), "col")
+    return jnp.sum(lax.all_gather(empty.at[row_blocks].add(terms), "col"), axis=0)
 
 
 def total_columns(terms, column_blocks, length):

time: 877 us -> 906 us (1.033)
  waiting for transfers between devices: 735 us -> 757 us
    all_gather x0 -> x1, waiting for transfers between devices: none -> 111 us  [total_rows(): lax.all_gather(empty.at[row_blocks].add(terms), 'col')]
    psum x1 -> x0, waiting for transfers between devices: 88.4 us -> none  [total_rows(): return lax.psum(empty.at[row_blocks].add(terms), 'col')]
where the time goes in v1:
time: 906 us; the launch traced here: 905 us
  waiting for transfers between devices  757 us (84%)
  other arithmetic  121 us (13%)
  between operations  15 us (2%)
  local copies, waits for them, and re-layouts  10.7 us (1%)
    pmax x4, waiting for transfers between devices, peak_rows(): return lax.pmax(empty.at[row_blocks].max(terms), 'col')  353 us
    pmax x4, waiting for transfers between devices, peak_columns(): return lax.pmax(empty.at[column_blocks].max(terms), 'row')  235 us
    all_gather x1, waiting for transfers between devices, total_rows(): lax.all_gather(empty.at[row_blocks].add(terms), 'col')  111 us
    reduce_max x4, other arithmetic, local_terms(): return (scaled.max(axis=2), scaled.max(axis=1))  60.2 us
    psum x1, waiting for transfers between devices, total_columns(): return lax.psum(empty.at[column_blocks].add(terms), 'row')  58 us
  transfers between devices with their start and end apart: 10, of which 10 were waited for; matrix products, arithmetic and copies ran while one was open for 3% of the time, Pallas kernels for 0%

profile of v1, /device:TPU:0, one launch (start us, length us, event | category | flops | bytes accessed | tf_op | source)
XLA Modules:
  0.0 904.6 jit_solution(18188700338756795221)
XLA Ops:
  7.9 0.7 fusion.30
  8.6 0.7 fusion.31
  9.3 1.1 gather_fusion.1
  10.5 1.1 gather_fusion
  11.6 15.0 %fusion.1 = (f32[288,128]{1,0:T(8,128)S(1)}, f32[288,128]{1,0:T(8,128)S(1)}) fusion(f32[288,128]{1,0:T(8,128)S(1)} %gather_fusion.1, f32[288,128]{1,0:T(8,128)S(1)} %gather_fusion, f32[1,1,288,128,128]{4,3,2,1,0:T(8,128)} %param.4, pred[288]{0:T(512)(128)(4,1)S(1)} %iota_compare_fusion), kind=kLoop, calls=%fused_computation.27 | loop fusion | flops 28237824 | bytes 19464480 | tf_op jit(solution)/shard_map/reduce_max | solution.py:14
  26.6 2.3 scatter_custom_fusion.1
  29.0 2.5 scatter_custom_fusion
  31.6 61.3 %all-reduce.12.cloned.1.call-done = f32[1024,128]{1,0:T(8,128)} async-done(((f32[1024,128]{1,0:T(8,128)}), f32[1024,128]{1,0:T(8,128)}) %all-reduce.12.cloned.1.call-update) | async-done | bytes 524304 | tf_op jit(solution)/shard_map/pmax | solution.py:25
  92.9 1.2 add_rsqrt_fusion.1
  94.1 1.1 gather_fusion.3
  95.2 88.2 %all-reduce.10.cloned.1.call-done = f32[2048,128]{1,0:T(8,128)} async-done(((f32[2048,128]{1,0:T(8,128)}), f32[2048,128]{1,0:T(8,128)}) %all-reduce.10.cloned.1.call-update) | async-done | bytes 1048592 | tf_op jit(solution)/shard_map/pmax | solution.py:20
  183.4 1.5 add_rsqrt_fusion
  184.9 1.1 gather_fusion.2
  185.9 15.0 %fusion.2 = (f32[288,128]{1,0:T(8,128)S(1)}, f32[288,128]{1,0:T(8,128)S(1)}) fusion(f32[288,128]{1,0:T(8,128)S(1)} %gather_fusion.3, f32[288,128]{1,0:T(8,128)S(1)} %gather_fusion.2, f32[1,1,288,128,128]{4,3,2,1,0:T(8,128)} %param.4, pred[288]{0:T(512)(128)(4,1)S(1)} %iota_compare_fusion), kind=kLoop, calls=%fused_computation.28 | loop fusion | flops 28237824 | bytes 19464480 | tf_op jit(solution)/shard_map/reduce_max | solution.py:14
  201.0 2.3 scatter_custom_fusion.3
  203.4 2.5 scatter_custom_fusion.2
  205.9 58.1 %all-reduce.16.cloned.1.call-done = f32[1024,128]{1,0:T(8,128)} async-done(((f32[1024,128]{1,0:T(8,128)}), f32[1024,128]{1,0:T(8,128)}) %all-reduce.16.cloned.1.call-update) | async-done | bytes 524304 | tf_op jit(solution)/shard_map/pmax | solution.py:25
  264.0 1.2 rsqrt_multiply_fusion.5
  265.2 1.1 gather_fusion.5
  266.3 88.1 %all-reduce.14.cloned.1.call-done = f32[2048,128]{1,0:T(8,128)} async-done(((f32[2048,128]{1,0:T(8,128)}), f32[2048,128]{1,0:T(8,128)}) %all-reduce.14.cloned.1.call-update) | async-done | bytes 1048592 | tf_op jit(solution)/shard_map/pmax | solution.py:20
  354.4 1.5 rsqrt_multiply_fusion.2
  355.9 1.1 gather_fusion.4
  357.0 15.0 %fusion.4 = (f32[288,128]{1,0:T(8,128)S(1)}, f32[288,128]{1,0:T(8,128)S(1)}) fusion(f32[288,128]{1,0:T(8,128)S(1)} %gather_fusion.5, f32[288,128]{1,0:T(8,128)S(1)} %gather_fusion.4, f32[1,1,288,128,128]{4,3,2,1,0:T(8,128)} %param.4, pred[288]{0:T(512)(128)(4,1)S(1)} %iota_compare_fusion), kind=kLoop, calls=%fused_computation.30 | loop fusion | flops 28237824 | bytes 19464480 | tf_op jit(solution)/shard_map/reduce_max | solution.py:14
  372.0 2.3 scatter_custom_fusion.5
  374.6 2.5 scatter_custom_fusion.4
  377.2 57.9 %all-reduce.20.cloned.1.call-done = f32[1024,128]{1,0:T(8,128)} async-done(((f32[1024,128]{1,0:T(8,128)}), f32[1024,128]{1,0:T(8,128)}) %all-reduce.20.cloned.1.call-update) | async-done | bytes 524304 | tf_op jit(solution)/shard_map/pmax | solution.py:25
  435.1 1.1 rsqrt_multiply_fusion.4
  436.2 1.1 gather_fusion.7
  437.2 88.2 %all-reduce.18.cloned.1.call-done = f32[2048,128]{1,0:T(8,128)} async-done(((f32[2048,128]{1,0:T(8,128)}), f32[2048,128]{1,0:T(8,128)}) %all-reduce.18.cloned.1.call-update) | async-done | bytes 1048592 | tf_op jit(solution)/shard_map/pmax | solution.py:20
  525.4 1.4 rsqrt_multiply_fusion.1
  526.8 1.1 gather_fusion.6
  527.8 15.0 %fusion.6 = (f32[288,128]{1,0:T(8,128)S(1)}, f32[288,128]{1,0:T(8,128)S(1)}) fusion(f32[288,128]{1,0:T(8,128)S(1)} %gather_fusion.7, f32[288,128]{1,0:T(8,128)S(1)} %gather_fusion.6, f32[1,1,288,128,128]{4,3,2,1,0:T(8,128)} %param.4, pred[288]{0:T(512)(128)(4,1)S(1)} %iota_compare_fusion), kind=kLoop, calls=%fused_computation.32 | loop fusion | flops 28237824 | bytes 19464480 | tf_op jit(solution)/shard_map/reduce_max | solution.py:14
  542.9 2.3 scatter_custom_fusion.7
  545.3 2.5 scatter_custom_fusion.6
  547.9 58.1 %all-reduce.24.cloned.1.call-done = f32[1024,128]{1,0:T(8,128)} async-done(((f32[1024,128]{1,0:T(8,128)}), f32[1024,128]{1,0:T(8,128)}) %all-reduce.24.cloned.1.call-update) | async-done | bytes 524304 | tf_op jit(solution)/shard_map/pmax | solution.py:25
  605.9 1.1 rsqrt_multiply_fusion.3
  607.1 1.1 gather_fusion.9
  608.1 88.3 %all-reduce.22.cloned.1.call-done = f32[2048,128]{1,0:T(8,128)} async-done(((f32[2048,128]{1,0:T(8,128)}), f32[2048,128]{1,0:T(8,128)}) %all-reduce.22.cloned.1.call-update) | async-done | bytes 1048592 | tf_op jit(solution)/shard_map/pmax | solution.py:20
  696.4 1.4 rsqrt_multiply_fusion
  697.8 1.1 gather_fusion.8
  698.9 15.1 %fusion.8 = (f32[288,128]{1,0:T(8,128)S(1)}, f32[288,128]{1,0:T(8,128)S(1)}) fusion(f32[288,128]{1,0:T(8,128)S(1)} %gather_fusion.9, f32[288,128]{1,0:T(8,128)S(1)} %gather_fusion.8, f32[1,1,288,128,128]{4,3,2,1,0:T(8,128)} %param.4, pred[288]{0:T(512)(128)(4,1)S(1)} %iota_compare_fusion), kind=kLoop, calls=%fused_computation.34 | loop fusion | flops 28237824 | bytes 19464480 | tf_op jit(solution)/shard_map/reduce_sum | solution.py:15
  714.0 2.3 scatter_custom_fusion.9
  716.4 2.5 scatter_custom_fusion.8
  718.9 58.0 %all-reduce.26.cloned.1.call-done = f32[1024,128]{1,0:T(8,128)} async-done(((f32[1024,128]{1,0:T(8,128)}), f32[1024,128]{1,0:T(8,128)}) %all-reduce.26.cloned.1.call-update) | async-done | bytes 524304 | tf_op jit(solution)/shard_map/psum | solution.py:35
  776.9 1.9 multiply_bitcast_fusion.1
  778.8 111.2 %all-gather.3.cloned.1.call-done = f32[32768,128]{1,0:T(8,128)} async-done(((f32[2048,128]{1,0:T(8,128)}), f32[32768,128]{1,0:T(8,128)}) %all-gather.3.cloned.1.call-update) | async-done | bytes 16777232 | tf_op jit(solution)/shard_map/all_gather | solution.py:30
  890.0 6.6 reduce_sum.28
  896.6 1.1 multiply_bitcast_fusion
  (29 shorter events, 0.9 us)
Async XLA Ops:
  7.2 85.7 %all-reduce.12.cloned.1.call-start = ((), (), s32[]{:S(2)}) async-start(), calls=%async_computation.1 | async-start | bytes 1048576 | tf_op jit(solution)/shard_map/pmax | solution.py:25
  28.9 154.5 %all-reduce.10.cloned.1.call-start = ((), (), s32[]{:S(2)}) async-start(), calls=%async_computation | async-start | bytes 2097152 | tf_op jit(solution)/shard_map/pmax | solution.py:20
  31.5 232.5 %all-reduce.16.cloned.1.call-start = ((), (), s32[]{:S(2)}) async-start(), calls=%async_computation.3 | async-start | bytes 1048576 | tf_op jit(solution)/shard_map/pmax | solution.py:25
  92.9 171.1 %copy-start.1 = (f32[1024,128]{1,0:T(8,128)S(1)}, f32[1024,128]{1,0:T(8,128)}, u32[]{:S(2)}) copy-start(f32[1024,128]{1,0:T(8,128)} %all-reduce.12.cloned.1.call-done) | copy-start | bytes 1572868
  183.4 171.0 %copy-start = (f32[2048,128]{1,0:T(8,128)S(1)}, f32[2048,128]{1,0:T(8,128)}, u32[]{:S(2)}) copy-start(f32[2048,128]{1,0:T(8,128)} %all-reduce.10.cloned.1.call-done) | copy-start | bytes 3145732
  203.3 151.1 %all-reduce.14.cloned.1.call-start = ((), (), s32[]{:S(2)}) async-start(), calls=%async_computation.2 | async-start | bytes 2097152 | tf_op jit(solution)/shard_map/pmax | solution.py:20
  205.9 229.2 %all-reduce.20.cloned.1.call-start = ((), (), s32[]{:S(2)}) async-start(), calls=%async_computation.5 | async-start | bytes 1048576 | tf_op jit(solution)/shard_map/pmax | solution.py:25
  374.3 151.1 %all-reduce.18.cloned.1.call-start = ((), (), s32[]{:S(2)}) async-start(), calls=%async_computation.4 | async-start | bytes 2097152 | tf_op jit(solution)/shard_map/pmax | solution.py:20
  377.1 228.8 %all-reduce.24.cloned.1.call-start = ((), (), s32[]{:S(2)}) async-start(), calls=%async_computation.7 | async-start | bytes 1048576 | tf_op jit(solution)/shard_map/pmax | solution.py:25
  545.2 151.2 %all-reduce.22.cloned.1.call-start = ((), (), s32[]{:S(2)}) async-start(), calls=%async_computation.6 | async-start | bytes 2097152 | tf_op jit(solution)/shard_map/pmax | solution.py:20
  547.8 229.1 %all-reduce.26.cloned.1.call-start = ((), (), s32[]{:S(2)}) async-start(), calls=%async_computation.8 | async-start | bytes 1048576 | tf_op jit(solution)/shard_map/psum | solution.py:35
  716.3 173.6 %all-gather.3.cloned.1.call-start = ((), (), s32[]{:S(2)}) async-start(), calls=%async_computation.9 | async-start | bytes 17825792 | tf_op jit(solution)/shard_map/all_gather | solution.py:30
Sparse Core Ops, SparseCore 0:
  29.1 63.8 all-reduce.11
  96.7 86.6 all-reduce.9
  203.4 60.5 all-reduce.15
  267.7 86.6 all-reduce.13
  374.5 60.5 all-reduce.19
  438.7 86.6 all-reduce.17
  545.3 60.5 all-reduce.23
  609.8 86.6 all-reduce.21
  716.4 60.3 all-reduce.25
  779.4 110.4 all-gather.2
